TPU v7x, 1024 devices: a whole 4x8x16 slice. The times are simulated.
1024 devices in a mesh: dp: 4 (over z_hi), pipe: 16 (over x, z_lo), expert: 16 (over y, core).
Axes of the slice: x: 4, y: 8, z: 16 (z_hi: 4, z_lo: 4; z = z_hi * 4 + z_lo), core: 2. Of those that a mesh axis runs over, the one named last changes fastest.
Arguments:
- output_grads: bfloat16 [4, 16, 2048, 4096], P('dp', 'pipe', 'expert'), may hold values from -4 to 4
- gate_values: float32 [4, 16, 2048, 8], P('dp', 'pipe', 'expert'), may hold values from 0.1 to 1
- routing: int32 [4, 16, 2048, 8], P('dp', 'pipe', 'expert'), may hold values from 0 to 127, as said below
- saved_inputs: bfloat16 [4, 16, 1, 16, 16, 4096], P('dp', 'pipe'), may hold values from -6 to 6
- expert_weights: bfloat16 [16, 3, 1536, 4096], P('pipe', None, 'expert'), may hold values from -0.09375 to 0.09375
Outputs:
- passed_grads: bfloat16 [4, 16, 2048, 4096], P('dp', 'pipe', 'expert')
- weight_grads: bfloat16 [16, 3, 1536, 4096], P('pipe', None, 'expert', 'dp')
Inputs may be any that keep to these rules, and one draw needn't show every extreme that they name: `routing`: each token names 8 different experts. Among the 128 tokens of one device (each aligned block of 128 tokens of a micro-batch), every expert below 1 is named by 1 to 16 tokens. In some replica and section, one such expert is named by exactly 16 tokens of every device of the expert axis.
All inputs are finite; a program needn't handle non-finite values.
Results may differ from a plain program's by a relative error of at most 0.014.
Values may be sent and summed in bfloat16 or wider, within the bound.
A program may use at most 32 MiB of HBM per device.

v0:
```python
import jax
import jax.numpy as jnp
from jax import lax
from jax.sharding import PartitionSpec as P


def shifted(value, axis, by):
    devices = lax.axis_size(axis)
    return lax.ppermute(value, axis, [(i, (i + by) % devices) for i in range(devices)])


def route_tables(routing, gate_values, flight, capacity):
    expert_index = jnp.arange(flight, dtype=jnp.int32)
    matches = routing[:, :, None] == expert_index[None, None, :]
    member = jnp.any(matches, axis=1)
    gate_share = jnp.sum(jnp.where(matches, gate_values[:, :, None], jnp.float32(0.0)), axis=1)
    member_count = member.astype(jnp.int32)
    slot_index = jnp.cumsum(member_count, axis=0) - member_count
    chooser = (
        slot_index[None, :, :] == jnp.arange(capacity, dtype=jnp.int32)[:, None, None]
    ) & member[None, :, :]
    selector = jnp.transpose(chooser, (2, 0, 1))
    return (member, slot_index, gate_share, selector)


def shards(output_grads, gate_values, routing, saved_inputs, expert_weights):
    owners = lax.axis_size("expert")
    flight = max(1, owners // 16)
    per_expert = owners // flight
    own_expert = lax.axis_index("expert") // per_expert
    capacity = saved_inputs.shape[4]
    incoming = output_grads[0, 0]
    width = incoming.shape[1]
    member, slot_index, gate_share, selector = route_tables(
        routing[0, 0], gate_values[0, 0], flight, capacity
    )
    picked = jnp.einsum(
        "ect,td->ecd", selector.astype(jnp.bfloat16), incoming, preferred_element_type=jnp.float32
    )
    weighting = jnp.sum(
        jnp.where(selector, jnp.transpose(gate_share)[:, None, :], jnp.float32(0.0)), axis=-1
    )
    routed = (picked * weighting[:, :, None]).astype(jnp.bfloat16)
    full_weights = expert_weights[0]
    outgoing = jnp.repeat(routed, per_expert, axis=0)
    arrived = lax.all_to_all(outgoing, "expert", split_axis=0, concat_axis=0, tiled=True)
    rows_count = owners * capacity
    own_inputs = lax.dynamic_index_in_dim(
        saved_inputs[0, 0], own_expert, 0, keepdims=False
    ).reshape(rows_count, width)
    routed_rows = arrived.reshape(rows_count, width)
    gate_weight = full_weights[0]
    up_weight = full_weights[1]
    down_weight = full_weights[2]
    contract = (((1,), (1,)), ((), ()))
    gate_pre = lax.dot_general(
        own_inputs, gate_weight, contract, preferred_element_type=jnp.float32
    )
    up_pre = lax.dot_general(own_inputs, up_weight, contract, preferred_element_type=jnp.float32)
    sigmoid_gate = jax.nn.sigmoid(gate_pre)
    activated = gate_pre * sigmoid_gate
    hidden = (activated * up_pre).astype(jnp.bfloat16)
    hidden_grad = lax.dot_general(
        routed_rows, down_weight, contract, preferred_element_type=jnp.float32
    )
    gate_grad = (
        hidden_grad * up_pre * sigmoid_gate * (1.0 + gate_pre * (1.0 - sigmoid_gate))
    ).astype(jnp.bfloat16)
    up_grad = (hidden_grad * activated).astype(jnp.bfloat16)
    partial_value = jnp.dot(gate_grad, gate_weight, preferred_element_type=jnp.float32) + jnp.dot(
        up_grad, up_weight, preferred_element_type=jnp.float32
    )
    partial_value = partial_value.astype(jnp.bfloat16).reshape(owners, capacity, width)
    returned = lax.all_to_all(partial_value, "expert", split_axis=0, concat_axis=0, tiled=True)
    summed = jnp.sum(
        returned.reshape(flight, per_expert, capacity, width).astype(jnp.float32), axis=1
    )
    summed_rows = summed.reshape(flight * capacity, width)
    lookup = jnp.arange(flight, dtype=jnp.int32)[None, :] * capacity + jnp.minimum(
        slot_index, capacity - 1
    )
    gathered = jnp.take(summed_rows, lookup, axis=0)
    added = jnp.sum(jnp.where(member[:, :, None], gathered, jnp.float32(0.0)), axis=1)
    input_grads = (incoming.astype(jnp.float32) + added).astype(jnp.bfloat16)
    passed_grads = shifted(input_grads, "pipe", -1)[None, None]
    by_rows = (((0,), (0,)), ((), ()))
    stacked = jnp.stack(
        [
            lax.dot_general(gate_grad, own_inputs, by_rows, preferred_element_type=jnp.float32),
            lax.dot_general(up_grad, own_inputs, by_rows, preferred_element_type=jnp.float32),
            lax.dot_general(hidden, routed_rows, by_rows, preferred_element_type=jnp.float32),
        ]
    )
    weight_total = lax.psum_scatter(
        stacked.astype(jnp.bfloat16), "dp", scatter_dimension=2, tiled=True
    )
    weight_grads = weight_total[None]
    return (passed_grads, weight_grads)


def solution(mesh):
    placed = (
        P("dp", "pipe", "expert", None),
        P("dp", "pipe", "expert", None),
        P("dp", "pipe", "expert", None),
        P("dp", "pipe", None, None, None, None),
        P("pipe", None, "expert", None),
    )
    return jax.shard_map(
        shards,
        mesh=mesh,
        in_specs=placed,
        out_specs=(P("dp", "pipe", "expert", None), P("pipe", None, "expert", "dp")),
        check_vma=False,
    )
```

profile of v0, /device:TPU:129, one launch (start us, length us, event | category | flops | bytes accessed | tf_op | source)
XLA Modules:
  0.0 224.1 jit_solution(2064432521256191616)
XLA Ops:
  7.2 0.0 copy-start
  7.2 0.9 fusion.31
  8.0 0.1 copy.9
  8.2 0.2 reduce_window_sum.15
  8.3 0.1 reduce.7
  8.5 0.7 select_reduce_fusion.1
  9.2 0.1 select_reduce_fusion
  9.3 1.5 fusion.4
  10.8 1.5 reshape.319
  12.3 7.8 %all-to-all-start = ((bf16[16,16,4096]{2,1,0:T(8,128)(2,1)}), bf16[16,16,4096]{2,1,0:T(8,128)(2,1)}, u32[]{:S(2)}, u32[]{:S(2)}) async-start(bf16[16,16,4096]{2,1,0:T(8,128)(2,1)} %reshape.319), calls=%async_computation | async-start | bytes 4194304 | tf_op jit(solution)/shard_map/all_to_all | solution.py:46
  20.1 1.9 fusion.8
  22.0 1.9 fusion.11
  23.9 45.3 %all-to-all-done = bf16[16,16,4096]{2,1,0:T(8,128)(2,1)} async-done(((bf16[16,16,4096]{2,1,0:T(8,128)(2,1)}), bf16[16,16,4096]{2,1,0:T(8,128)(2,1)}, u32[]{:S(2)}, u32[]{:S(2)}) %all-to-all-start) | async-done | bytes 2097184 | tf_op jit(solution)/shard_map/all_to_all | solution.py:46
  69.2 2.7 %multiply_convert_fusion.1 = (bf16[256,96]{0,1:T(8,128)(2,1)S(1)}, bf16[256,96]{0,1:T(8,128)(2,1)S(1)}) fusion(f32[256,96]{0,1:T(8,128)S(1)} %fusion.8, f32[256,96]{0,1:T(8,128)S(1)} %fusion.11, bf16[256,4096]{1,0:T(8,128)(2,1)} %bitcast.3, bf16[1,3,96,4096]{3,2,1,0:T(8,128)(2,1)} %param.9), kind=kOutput, calls=%fused_computation.30 | convolution fusion | flops 201646080 | bytes 3178496 | tf_op jit(solution)/shard_map/dot_general | solution.py:63
  72.0 0.7 fusion.6
  72.7 2.1 fusion
  74.8 4.8 %all-to-all-start.1 = ((bf16[16,16,4096]{2,1,0:T(8,128)(2,1)}), bf16[16,16,4096]{2,1,0:T(8,128)(2,1)}, u32[]{:S(2)}, u32[]{:S(2)}) async-start(bf16[16,16,4096]{2,1,0:T(8,128)(2,1)} %bitcast.59), calls=%async_computation.1 | async-start | bytes 4194304 | tf_op jit(solution)/shard_map/all_to_all | solution.py:74
  79.6 0.0 reduce-scatter.2.cloned.1.call-start
  79.7 0.5 fusion.2
  80.1 0.5 fusion.1
  80.6 2.1 fusion.3
  82.7 1.7 pad_maximum_fusion
  84.3 0.0 reduce-scatter.2.cloned.1.call-update
  84.4 44.7 %all-to-all-done.1 = bf16[16,16,4096]{2,1,0:T(8,128)(2,1)} async-done(((bf16[16,16,4096]{2,1,0:T(8,128)(2,1)}), bf16[16,16,4096]{2,1,0:T(8,128)(2,1)}, u32[]{:S(2)}, u32[]{:S(2)}) %all-to-all-start.1) | async-done | bytes 2097184 | tf_op jit(solution)/shard_map/all_to_all | solution.py:74
  129.1 1.9 convert_reduce_fusion
  131.0 0.0 copy-start.1
  131.0 2.5 %gather_fusion = f32[128,4096]{1,0:T(8,128)} fusion(f32[16,4096]{1,0:T(8,128)S(1)} %convert_reduce_fusion, s32[1024]{0:T(1024)S(1)} %pad_clamp_fusion), kind=kCustom, calls=%fused_computation | custom fusion | bytes 4194816 | tf_op jit(solution)/shard_map/jit(_take)/gather | solution.py:82
  133.5 2.0 add_convert_fusion
  135.6 1.9 collective-permute-start
  137.5 75.1 %collective-permute-done = bf16[128,4096]{1,0:T(8,128)(2,1)S(1)} collective-permute-done((bf16[128,4096]{1,0:T(8,128)(2,1)S(1)}, bf16[128,4096]{1,0:T(8,128)(2,1)S(1)}, u32[]{:S(2)}, u32[]{:S(2)}) %collective-permute-start) | collective-permute-done | bytes 1048608 | tf_op jit(solution)/shard_map/ppermute | solution.py:9
  212.6 3.7 %reduce-scatter.2.cloned.1.call-done = bf16[3,96,1024]{2,1,0:T(8,128)(2,1)} async-done(((bf16[3,96,4096]{2,1,0:T(8,128)(2,1)}), bf16[3,96,1024]{2,1,0:T(8,128)(2,1)}) %reduce-scatter.2.cloned.1.call-update) | async-done | bytes 589840 | tf_op jit(solution)/shard_map/reduce_scatter | solution.py:94
  216.3 1.0 copy.11
  (8 shorter events, 0.0 us)
Async XLA Ops:
  7.2 12.9 %copy-start = (bf16[1,1,1,16,16,4096]{5,4,3,2,1,0:T(8,128)(2,1)S(1)}, bf16[1,1,1,16,16,4096]{5,4,3,2,1,0:T(8,128)(2,1)}, u32[]{:S(2)}) copy-start(bf16[1,1,1,16,16,4096]{5,4,3,2,1,0:T(8,128)(2,1)} %param.8) | copy-start | bytes 6291460
  12.3 56.9 %all-to-all-start = ((bf16[16,16,4096]{2,1,0:T(8,128)(2,1)}), bf16[16,16,4096]{2,1,0:T(8,128)(2,1)}, u32[]{:S(2)}, u32[]{:S(2)}) async-start(bf16[16,16,4096]{2,1,0:T(8,128)(2,1)} %reshape.319), calls=%async_computation | async-start | bytes 4194304 | tf_op jit(solution)/shard_map/all_to_all | solution.py:46
  69.2 2.7 %copy-start.2 = (bf16[1,3,96,4096]{3,2,1,0:T(8,128)(2,1)S(1)}, bf16[1,3,96,4096]{3,2,1,0:T(8,128)(2,1)}, u32[]{:S(2)}) copy-start(bf16[1,3,96,4096]{3,2,1,0:T(8,128)(2,1)} %param.9) | copy-start | bytes 7077892
  74.8 54.3 %all-to-all-start.1 = ((bf16[16,16,4096]{2,1,0:T(8,128)(2,1)}), bf16[16,16,4096]{2,1,0:T(8,128)(2,1)}, u32[]{:S(2)}, u32[]{:S(2)}) async-start(bf16[16,16,4096]{2,1,0:T(8,128)(2,1)} %bitcast.59), calls=%async_computation.1 | async-start | bytes 4194304 | tf_op jit(solution)/shard_map/all_to_all | solution.py:74
  79.6 136.7 %reduce-scatter.2.cloned.1.call-start = ((), (), s32[]{:S(2)}) async-start(), calls=%async_computation.3 | async-start | bytes 2949120 | tf_op jit(solution)/shard_map/reduce_scatter | solution.py:94
  131.0 2.5 %copy-start.1 = (bf16[1,1,128,4096]{3,2,1,0:T(8,128)(2,1)S(1)}, bf16[1,1,128,4096]{3,2,1,0:T(8,128)(2,1)}, u32[]{:S(2)}) copy-start(bf16[1,1,128,4096]{3,2,1,0:T(8,128)(2,1)} %param.5) | copy-start | bytes 3145732
  135.6 77.0 %collective-permute-start = (bf16[128,4096]{1,0:T(8,128)(2,1)S(1)}, bf16[128,4096]{1,0:T(8,128)(2,1)S(1)}, u32[]{:S(2)}, u32[]{:S(2)}) collective-permute-start(bf16[128,4096]{1,0:T(8,128)(2,1)S(1)} %add_convert_fusion), channel_id=1, source_target_pairs={{0,240},{16,0},{32,16},{48,32},{64,48},{80,64},{96,80},{112,96},{1... | collective-permute-start | bytes 3145736 | tf_op jit(solution)/shard_map/ppermute | solution.py:9
Sparse Core Ops, SparseCore 0:
  84.5 131.7 reduce-scatter.1
where the time goes:
time: 225 us; the launch traced here: 224 us
  waiting for transfers between devices  169 us (75%)
  starting transfers between devices  14.6 us (6%)
  between operations  14.1 us (6%)
  matrix products  13.8 us (6%)
  other arithmetic  7.62 us (3%)
  local copies, waits for them, and re-layouts  5.17 us (2%)
    ppermute x1, waiting for transfers between devices, shifted(): lax.ppermute(value, axis, [(i, (i + by) % devices) for i in range(devices)])  75.1 us
    all_to_all x1, waiting for transfers between devices, shards(): lax.all_to_all(outgoing, 'expert', split_axis=0, concat_axis=0, tiled=True)  45.3 us
    all_to_all x1, waiting for transfers between devices, shards(): lax.all_to_all(partial_value, 'expert', split_axis=0, concat_axis=0, tile...  44.7 us
    all_to_all x1, starting transfers between devices, shards(): lax.all_to_all(outgoing, 'expert', split_axis=0, concat_axis=0, tiled=True)  7.79 us
    all_to_all x1, starting transfers between devices, shards(): lax.all_to_all(partial_value, 'expert', split_axis=0, concat_axis=0, tile...  4.85 us
  transfers between devices with their start and end apart: 4, of which 4 were waited for; matrix products, arithmetic and copies ran while one was open for 7% of the time, Pallas kernels for 0%

commit v1 on v0

v1 whole, which is shorter than its diff:
```python
import functools

import jax
import jax.numpy as jnp
from jax import lax
from jax.experimental import pallas as pl
from jax.experimental.pallas import tpu as pltpu
from jax.sharding import PartitionSpec as P

MESH = pl.DeviceIdType.MESH
BF16 = jnp.bfloat16
F32 = jnp.float32
NT = (((1,), (1,)), ((), ()))
TN = (((0,), (0,)), ((), ()))


def one_hot(routing, capacity):
    tokens = routing.shape[1]
    hit = routing == 0
    member = jnp.max(jnp.where(hit, F32(1.0), F32(0.0)), axis=0, keepdims=True)
    before = lax.broadcasted_iota(jnp.int32, (tokens, tokens), 0) < lax.broadcasted_iota(
        jnp.int32, (tokens, tokens), 1
    )
    upper = jnp.where(before, F32(1.0), F32(0.0)).astype(BF16)
    rows = jnp.broadcast_to(member, (capacity, tokens))
    slot = jnp.dot(rows.astype(BF16), upper, preferred_element_type=F32)
    index = lax.broadcasted_iota(jnp.int32, (capacity, tokens), 0).astype(F32)
    return hit, jnp.where((slot == index) & (rows > 0.5), F32(1.0), F32(0.0))


def kernel(
    n_y, n_dp, n_pipe,
    routing_ref, gates_ref, og_hbm, x_hbm, w_hbm,
    passed_ref, grads_ref,
    og, x, w_gu, w_d, rows_all, picked, slices, relay, acts, acts_in, both, wide, part,
    ring_in, ring_out, og_in, routing_in, final, final_in, acc_gu, acc_d, act_g, act_u,
    load_sem, og_send, og_recv, rt_send, rt_recv, fin_send, fin_recv, w_send, w_recv,
    y_send, y_recv, ysib_send, ysib_recv, s_send, s_recv, ssib_send, ssib_recv,
    xy_send, xy_recv, rl_send, rl_recv, rf_send, rf_recv,
    h_send, h_recv, hf_send, hf_recv, g_send, g_recv, gf_send, gf_recv,
    t_send, t_recv, r_send, r_recv,
):
    dp = lax.axis_index("dp")
    pipe = lax.axis_index("pipe")
    expert = lax.axis_index("expert")
    y = expert // 2
    core = expert % 2
    far = n_y // 2
    cap, width = rows_all.shape[1], rows_all.shape[2]
    half = width // 2
    hid = w_d.shape[0]
    tokens = og.shape[0]
    part_d = width // n_dp
    tile = width // 8
    sib = {"expert": y * 2 + (1 - core)}
    y_to = ({"expert": ((y + 1) % n_y) * 2 + core}, {"expert": ((y + n_y - 1) % n_y) * 2 + core})
    d_to = ({"dp": (dp + 1) % n_dp}, {"dp": (dp + n_dp - 1) % n_dp})
    p_to = {"pipe": (pipe + n_pipe - 1) % n_pipe}
    p_from = {"pipe": (pipe + 1) % n_pipe}

    sent = []

    def send(src, dst, ssem, rsem, to):
        copy = pltpu.make_async_remote_copy(
            src_ref=src, dst_ref=dst, send_sem=ssem, recv_sem=rsem, device_id=to,
            device_id_type=MESH,
        )
        copy.start()
        sent.append(copy)

    def arrived(dst, rsem, to):
        pltpu.make_async_remote_copy(
            src_ref=dst, dst_ref=dst, send_sem=rsem, recv_sem=rsem, device_id=to,
            device_id_type=MESH,
        ).wait_recv()

    loads = [
        pltpu.make_async_copy(og_hbm, og, load_sem.at[0]),
        pltpu.make_async_copy(x_hbm, x, load_sem.at[1]),
        pltpu.make_async_copy(w_hbm.at[pl.ds(0, 2)], w_gu.at[core], load_sem.at[2]),
        pltpu.make_async_copy(w_hbm.at[2], w_d, load_sem.at[3]),
    ]
    barrier = pltpu.get_barrier_semaphore()
    peers = (sib, *y_to, *d_to, p_to, p_from)
    for peer in peers:
        pl.semaphore_signal(barrier, inc=1, device_id=peer, device_id_type=MESH)
    for load in loads:
        load.start()

    hit, chooser = one_hot(routing_ref[...], cap)
    share = jnp.sum(jnp.where(hit, gates_ref[...], F32(0.0)), axis=0, keepdims=True)
    weighting = jnp.sum(chooser * share, axis=1, keepdims=True)
    chooser = chooser.astype(BF16)
    loads[0].wait()
    for at in range(4):
        cols = pl.ds(at * (width // 4), width // 4)
        chosen = jnp.dot(chooser, og[:, cols], preferred_element_type=F32)
        picked[:, cols] = chosen
        rows_all[expert, :, cols] = (chosen * weighting).astype(BF16)
    pl.semaphore_wait(barrier, len(peers))

    def gather(piece, ring_send, ring_recv, sib_send, sib_recv):
        def owner(offset):
            return ((y + offset + n_y) % n_y) * 2 + core

        def first():
            for d, order in ((0, (0, 1)), (1, (1, 0))):
                for h in order:
                    send(piece(expert, h), piece(expert, h), ring_send.at[d, 0, h],
                         ring_recv.at[d, 0, h], y_to[d])
            for h in (0, 1):
                send(piece(expert, h), piece(expert, h), sib_send.at[0, h], sib_recv.at[0, h], sib)

        def step(k):
            for at in (0, 1):
                for d in (0, 1):
                    h = at if d == 0 else 1 - at
                    if k == far and at == 1:
                        continue
                    offset = -k if d == 0 else k
                    block = piece(owner(offset), h)
                    arrived(block, ring_recv.at[d, k - 1, h], y_to[d])
                    if k < far - 1 or (k == far - 1 and at == 0):
                        send(block, block, ring_send.at[d, k, h], ring_recv.at[d, k, h], y_to[d])
                    slot = offset % n_y
                    send(block, block, sib_send.at[slot, h], sib_recv.at[slot, h], sib)

        def finish():
            for offset in range(n_y):
                for h in (0, 1):
                    other = ((y + offset) % n_y) * 2 + (1 - core)
                    arrived(piece(other, h), sib_recv.at[offset, h], sib)

        return first, step, finish

    ag_first, ag_step, ag_finish = gather(
        lambda e, h: rows_all.at[e, :, pl.ds(h * half, half)], y_send, y_recv, ysib_send, ysib_recv
    )
    sl_first, sl_step, sl_finish = gather(
        lambda e, h: slices.at[e, pl.ds(3 * h, 3)], s_send, s_recv, ssib_send, ssib_recv
    )

    def send_slices(src, kind):
        for d in (0, 1):
            peer = (dp + 1) % n_dp if d == 0 else (dp + n_dp - 1) % n_dp
            near = pl.ds(pl.multiple_of(peer * part_d, part_d), part_d)
            send(src.at[expert, :, near], slices.at[expert, 3 * kind + d],
                 xy_send.at[kind, d], xy_recv.at[kind, d], d_to[d])
            base = ((dp + 2) % n_dp) * part_d + d * (part_d // 2)
            beyond = pl.ds(pl.multiple_of(base, part_d // 2), part_d // 2)
            send(src.at[expert, :, beyond], relay.at[d, kind],
                 rl_send.at[kind, d], rl_recv.at[kind, d], d_to[d])

    def relay_slices(kind):
        for d in (0, 1):
            arrived(relay.at[d, kind], rl_recv.at[kind, d], d_to[d])
            send(relay.at[d, kind],
                 slices.at[expert, 3 * kind + 2, :, pl.ds(d * (part_d // 2), part_d // 2)],
                 rf_send.at[kind, d], rf_recv.at[kind, d], d_to[d])

    def slices_arrived(kind):
        for d in (0, 1):
            arrived(slices.at[expert, 3 * kind + d], xy_recv.at[kind, d], d_to[d])
            arrived(slices.at[expert, 3 * kind + 2, :, pl.ds(d * (part_d // 2), part_d // 2)],
                    rf_recv.at[kind, d], d_to[d])

    og_rows = tokens // 4

    def send_og(at):
        block = pl.ds(at * og_rows, og_rows)
        send(og_hbm.at[block], og_in.at[block], og_send.at[at], og_recv.at[at], p_to)

    ag_first()
    send_slices(x_hbm, 0)
    send_slices(rows_all, 1)
    send(routing_ref, routing_in, rt_send, rt_recv, p_to)
    send(w_hbm.at[pl.ds(0, 2)], w_gu.at[core], w_send, w_recv, sib)
    send_og(0)

    loads[1].wait()
    loads[2].wait()

    def into(weights, rows_ref, out_rows):
        def body(at, total):
            cols = pl.ds(pl.multiple_of(at * tile, tile), tile)
            rows = rows_ref[:, :, cols].reshape(-1, tile)
            return total + lax.dot_general(weights(cols), rows, NT, preferred_element_type=F32)
        rows = rows_ref.shape[0] * rows_ref.shape[1]
        return lax.fori_loop(0, width // tile, body, jnp.zeros((out_rows, rows), F32))

    pre = into(lambda cols: w_gu[core, :, :, cols].reshape(2 * hid, tile), x, 2 * hid)
    gate_pre, up_pre = pre[:hid], pre[hid:]
    sigmoid = jax.nn.sigmoid(gate_pre)
    activated = gate_pre * sigmoid
    acts[0:hid, :] = (activated * up_pre).astype(BF16)
    act_g[...] = up_pre * sigmoid * (1.0 + gate_pre * (1.0 - sigmoid))
    act_u[...] = activated
    hidden_rows = pl.ds(0, hid)
    for d in (0, 1):
        send(acts.at[hidden_rows], acts_in.at[d, hidden_rows], h_send.at[d], h_recv.at[d], d_to[d])
    send_og(1)
    send_og(2)

    def relay_hidden():
        for d in (0, 1):
            arrived(acts_in.at[d, hidden_rows], h_recv.at[d], d_to[d])
            rows = pl.ds(d * (hid // 2), hid // 2)
            send(acts_in.at[d, rows], acts_in.at[2, rows], hf_send.at[d], hf_recv.at[d], d_to[d])

    for k in range(1, far):
        ag_step(k)
        if k == 1:
            relay_slices(0)
            relay_slices(1)
    slices_arrived(0)
    slices_arrived(1)
    sl_first()
    relay_hidden()
    ag_step(far)
    ag_finish()

    loads[3].wait()
    hidden_grad = into(lambda cols: w_d[:, cols], rows_all, hid)
    gate_grad = (hidden_grad * act_g[...]).astype(BF16)
    up_grad = (hidden_grad * act_u[...]).astype(BF16)
    acts[hid:2 * hid, :] = gate_grad
    acts[2 * hid:3 * hid, :] = up_grad
    both[core, 0:hid, :] = gate_grad
    both[core, hid:2 * hid, :] = up_grad
    send(acts.at[pl.ds(hid, 2 * hid)], both.at[core], t_send, t_recv, sib)
    for at in (0, 1):
        for d in (0, 1):
            m = at if d == 0 else 1 - at
            rows = pl.ds((1 + m) * hid, hid)
            send(acts.at[rows], acts_in.at[d, rows], g_send.at[d, m], g_recv.at[d, m], d_to[d])
    send_og(3)

    def relay_grads():
        for d in (0, 1):
            rows = pl.ds((1 + d) * hid, hid)
            arrived(acts_in.at[d, rows], g_recv.at[d, d], d_to[d])
            send(acts_in.at[d, rows], acts_in.at[2, rows], gf_send.at[d], gf_recv.at[d], d_to[d])

    arrived(both.at[1 - core], t_recv, sib)
    arrived(w_gu.at[1 - core], w_recv, sib)
    turned = jnp.transpose(both[...].reshape(4 * hid, rows_all.shape[0] * cap).astype(F32))
    wide[...] = turned.reshape(n_y, 2, cap, 4 * hid)
    mine = wide[:, core].reshape(n_y * cap, 4 * hid).astype(BF16)

    def partials(h):
        def body(at, carry):
            cols = pl.ds(pl.multiple_of(h * half + at * tile, tile), tile)
            weights = w_gu[:, :, :, cols].reshape(4 * hid, tile)
            part[:, :, cols] = jnp.dot(mine, weights, preferred_element_type=F32).reshape(
                n_y, cap, tile
            )
            return carry
        lax.fori_loop(0, half // tile, body, 0)

    def rs_send(d, k, h):
        cols = pl.ds(h * half, half)
        dest = (y + (k if d == 0 else -k) + n_y) % n_y
        value = part[dest, :, cols]
        if k < far and not (k == far - 1 and h != d):
            arrived(ring_in.at[d, k, :, cols], r_recv.at[d, k, h], y_to[d])
            value = value + ring_in[d, k, :, cols].astype(F32)
        ring_out[d, k - 1, :, cols] = value.astype(BF16)
        send(ring_out.at[d, k - 1, :, cols], ring_in.at[d, k - 1, :, cols],
             r_send.at[d, k - 1, h], r_recv.at[d, k - 1, h], y_to[d])

    def rs_step(k):
        for at in (1, 0) if k == far - 1 else (0, 1):
            for d in (0, 1):
                rs_send(d, k, at if d == 0 else 1 - at)

    def add_grads(j, gate_up, down):
        own = j is None
        base = pl.multiple_of(dp * part_d, part_d)
        cell = part_d // 2
        for at in (0, 1):
            cols = pl.ds(at * cell, cell)
            here = pl.ds(pl.multiple_of(base + at * cell, cell), cell)
            if gate_up:
                left = acts[hid:3 * hid, :] if own else acts_in[j, hid:3 * hid, :]
                right = x[:, :, here] if own else slices[:, j, :, cols]
                value = jnp.dot(left, right.reshape(-1, cell), preferred_element_type=F32)
                acc_gu[:, cols] = value if own else acc_gu[:, cols] + value
            if down:
                left = acts[0:hid, :] if own else acts_in[j, 0:hid, :]
                right = rows_all[:, :, here] if own else slices[:, 3 + j, :, cols]
                value = jnp.dot(left, right.reshape(-1, cell), preferred_element_type=F32)
                acc_d[:, cols] = value if own else acc_d[:, cols] + value

    partials(0)
    rs_send(0, far, 0)
    partials(1)
    rs_send(1, far, 1)
    sl_step(1)
    for k in range(far - 1, 0, -1):
        rs_step(k)
        if k == far - 1:
            add_grads(None, True, True)
        if k == far - 2 or far < 3:
            relay_grads()
        if far - k + 1 <= far:
            sl_step(far - k + 1)

    for h in (0, 1):
        cols = pl.ds(h * half, half)
        for d in (0, 1):
            if far > 1 or h == d:
                arrived(ring_in.at[d, 0, :, cols], r_recv.at[d, 0, h], y_to[d])
        total = part[y, :, cols] + (ring_in[0, 0, :, cols].astype(F32) + ring_in[1, 0, :, cols].astype(F32))
        final[:, cols] = (picked[:, cols] + total).astype(BF16)
        send(final.at[:, cols], final_in.at[:, cols], fin_send.at[h], fin_recv.at[h], p_to)

    sl_finish()
    for d in (0, 1):
        rows = pl.ds(d * (hid // 2), hid // 2)
        arrived(acts_in.at[2, rows], hf_recv.at[d], d_to[d])
    for j in range(3):
        add_grads(j, False, True)
    for d in (0, 1):
        rows = pl.ds((2 - d) * hid, hid)
        arrived(acts_in.at[d, rows], g_recv.at[d, 1 - d], d_to[d])
        add_grads(d, True, False)

    arrived(routing_in, rt_recv, p_to)
    _, placed = one_hot(routing_in[...], cap)
    placed = placed.astype(BF16)
    named = lax.dot_general(
        placed, jnp.ones((cap, 128), BF16), TN, preferred_element_type=F32
    )[:, 0:1] > 0.5
    for at in range(4):
        block = pl.ds(at * og_rows, og_rows)
        arrived(og_in.at[block], og_recv.at[at], p_to)
    for h in (0, 1):
        arrived(final_in.at[:, pl.ds(h * half, half)], fin_recv.at[h], p_to)
    for at in range(4):
        cols = pl.ds(at * (width // 4), width // 4)
        value = lax.dot_general(placed, final_in[:, cols], TN, preferred_element_type=F32)
        passed_ref[:, cols] = jnp.where(named, value, og_in[:, cols].astype(F32)).astype(BF16)

    for d in (0, 1):
        rows = pl.ds((1 + d) * hid, hid)
        arrived(acts_in.at[2, rows], gf_recv.at[d], d_to[d])
    add_grads(2, True, False)
    grads_ref[0] = acc_gu[0:hid, :].astype(BF16)
    grads_ref[1] = acc_gu[hid:2 * hid, :].astype(BF16)
    grads_ref[2] = acc_d[...].astype(BF16)
    for copy in sent:
        copy.wait_send()


def shards(output_grads, gate_values, routing, saved_inputs, expert_weights):
    n_dp, n_pipe = lax.axis_size("dp"), lax.axis_size("pipe")
    devices = lax.axis_size("expert")
    n_y = devices // 2
    far = n_y // 2
    cap, width = saved_inputs.shape[4], saved_inputs.shape[5]
    tokens = output_grads.shape[2]
    hid = expert_weights.shape[2]
    rows = devices * cap
    part_d = width // n_dp
    DMA = pltpu.SemaphoreType.DMA
    V = pltpu.VMEM
    scratch = [
        V((tokens, width), BF16),
        V((devices, cap, width), BF16),
        V((2, 2, hid, width), BF16),
        V((hid, width), BF16),
        V((devices, cap, width), BF16),
        V((cap, width), F32),
        V((devices, 6, cap, part_d), BF16),
        V((2, 2, cap, part_d // 2), BF16),
        V((3 * hid, rows), BF16),
        V((3, 3 * hid, rows), BF16),
        V((2, 2 * hid, rows), BF16),
        V((n_y, 2, cap, 4 * hid), F32),
        V((n_y, cap, width), F32),
        V((2, far, cap, width), BF16),
        V((2, far, cap, width), BF16),
        V((tokens, width), BF16),
        V(routing.shape[:1:-1], jnp.int32),
        V((cap, width), BF16),
        V((cap, width), BF16),
        V((2 * hid, part_d), F32),
        V((hid, part_d), F32),
        V((hid, rows), F32),
        V((hid, rows), F32),
        DMA((4,)), DMA((4,)), DMA((4,)), DMA, DMA, DMA((2,)), DMA((2,)), DMA, DMA,
        DMA((2, far, 2)), DMA((2, far, 2)), DMA((n_y, 2)), DMA((n_y, 2)),
        DMA((2, far, 2)), DMA((2, far, 2)), DMA((n_y, 2)), DMA((n_y, 2)),
        DMA((2, 2)), DMA((2, 2)), DMA((2, 2)), DMA((2, 2)), DMA((2, 2)), DMA((2, 2)),
        DMA((2,)), DMA((2,)), DMA((2,)), DMA((2,)), DMA((2, 2)), DMA((2, 2)), DMA((2,)), DMA((2,)),
        DMA, DMA, DMA((2, far, 2)), DMA((2, far, 2)),
    ]
    vmem = pl.BlockSpec(memory_space=pltpu.VMEM)
    anywhere = pl.BlockSpec(memory_space=pl.ANY)
    passed, grads = pl.pallas_call(
        functools.partial(kernel, n_y, n_dp, n_pipe),
        out_shape=(
            jax.ShapeDtypeStruct((tokens, width), BF16),
            jax.ShapeDtypeStruct((3, hid, part_d), BF16),
        ),
        in_specs=[vmem, vmem, anywhere, anywhere, anywhere],
        out_specs=(vmem, vmem),
        scratch_shapes=scratch,
        compiler_params=pltpu.CompilerParams(
            collective_id=0, has_side_effects=True, vmem_limit_bytes=48 << 20
        ),
        name="expert_backward",
    )(
        jnp.transpose(routing[0, 0]),
        jnp.transpose(gate_values[0, 0]),
        output_grads[0, 0],
        saved_inputs[0, 0, 0],
        expert_weights[0],
    )
    return passed[None, None], grads[None]


def solution(mesh):
    placed = (
        P("dp", "pipe", "expert", None),
        P("dp", "pipe", "expert", None),
        P("dp", "pipe", "expert", None),
        P("dp", "pipe", None, None, None, None),
        P("pipe", None, "expert", None),
    )
    return jax.shard_map(
        shards,
        mesh=mesh,
        in_specs=placed,
        out_specs=(P("dp", "pipe", "expert", None), P("pipe", None, "expert", "dp")),
        check_vma=False,
    )
```

time: 225 us -> 103 us (0.46)
  the two profiles are of different devices: /device:TPU:129 before, /device:TPU:78 now
where the time goes in v1:
time: 103 us
  Pallas kernels  96 us (93%)
  local copies, waits for them, and re-layouts  5.97 us (6%)
    pallas_call x1, Pallas kernels, shards(): pl.pallas_call(functools.partial(kernel, n_y, n_dp, n_pipe), out_shape=(j...  96 us
    unnamed x10, local copies, waits for them, and re-layouts  5.97 us

profile of v1, /device:TPU:78, one launch (start us, length us, event | category | flops | bytes accessed | tf_op | source)
XLA Modules:
  0.0 102.6 jit_solution(7735036619453931429)
XLA Ops:
  0.6 0.0 copy-start
  0.6 1.6 %copy-done = bf16[1,1,1,16,16,4096]{5,4,3,2,1,0:T(8,128)(2,1)S(1)} copy-done((bf16[1,1,1,16,16,4096]{5,4,3,2,1,0:T(8,128)(2,1)S(1)}, bf16[1,1,1,16,16,4096]{5,4,3,2,1,0:T(8,128)(2,1)}, u32[]{:S(2)}) %copy-start) | copy-done | bytes 2097176
  2.2 0.0 copy-start.1
  2.2 1.2 %copy-done.1 = bf16[1,1,128,4096]{3,2,1,0:T(8,128)(2,1)S(1)} copy-done((bf16[1,1,128,4096]{3,2,1,0:T(8,128)(2,1)S(1)}, bf16[1,1,128,4096]{3,2,1,0:T(8,128)(2,1)}, u32[]{:S(2)}) %copy-start.1) | copy-done | bytes 1048600
  3.4 0.0 copy-start.2
  3.5 0.7 copy-done.2
  4.1 0.0 copy-start.3
  4.1 0.7 copy-done.3
  4.8 96.0 %expert_backward.1 = (bf16[128,4096]{1,0:T(8,128)(2,1)S(1)}, bf16[3,96,1024]{2,1,0:T(8,128)(2,1)S(1)}) custom-call(s32[8,128]{1,0:T(8,128)S(1)} %bitcast.15, f32[8,128]{1,0:T(8,128)S(1)} %bitcast.16, bf16[128,4096]{1,0:T(8,128)(2,1)S(1)} %bitcast.13, bf16[16,16,4096]{2,1,0:T(8,128)(2,1)S(1)} %bitcast.11, bf16[3,96,4096]{2,1,0:T(8,128)(2,1)} %bitcast.17), custom_call_target="tpu_custom_call" | custom-call | tf_op jit(solution)/shard_map/expert_backward/pallas_call | solution.py:400
  100.9 1.0 copy.9
  101.8 0.8 copy.10
Async XLA Ops:
  0.6 1.6 %copy-start = (bf16[1,1,1,16,16,4096]{5,4,3,2,1,0:T(8,128)(2,1)S(1)}, bf16[1,1,1,16,16,4096]{5,4,3,2,1,0:T(8,128)(2,1)}, u32[]{:S(2)}) copy-start(bf16[1,1,1,16,16,4096]{5,4,3,2,1,0:T(8,128)(2,1)} %param.8) | copy-start | bytes 6291460
  2.2 1.2 %copy-start.1 = (bf16[1,1,128,4096]{3,2,1,0:T(8,128)(2,1)S(1)}, bf16[1,1,128,4096]{3,2,1,0:T(8,128)(2,1)}, u32[]{:S(2)}) copy-start(bf16[1,1,128,4096]{3,2,1,0:T(8,128)(2,1)} %param.5) | copy-start | bytes 3145732
  3.4 0.7 copy-start.2
  4.1 0.7 copy-start.3

commit v2 on v1

--- a/solution.py
+++ b/solution.py
@@ -30,9 +30,9 @@
 
 def kernel(
     n_y, n_dp, n_pipe,
-    routing_ref, gates_ref, og_hbm, x_hbm, w_hbm,
+    routing_hbm, gates_hbm, og_hbm, x_hbm, w_hbm,
     passed_ref, grads_ref,
-    og, x, w_gu, w_d, rows_all, picked, slices, relay, acts, acts_in, both, wide, part,
+    routing_ref, gates_ref, og, x, w_gu, w_d, rows_all, picked, slices, relay, acts, acts_in, both, wide, part,
     ring_in, ring_out, og_in, routing_in, final, final_in, acc_gu, acc_d, act_g, act_u,
     load_sem, og_send, og_recv, rt_send, rt_recv, fin_send, fin_recv, w_send, w_recv,
     y_send, y_recv, ysib_send, ysib_recv, s_send, s_recv, ssib_send, ssib_recv,
@@ -79,14 +79,18 @@
         pltpu.make_async_copy(x_hbm, x, load_sem.at[1]),
         pltpu.make_async_copy(w_hbm.at[pl.ds(0, 2)], w_gu.at[core], load_sem.at[2]),
         pltpu.make_async_copy(w_hbm.at[2], w_d, load_sem.at[3]),
+        pltpu.make_async_copy(routing_hbm, routing_ref, load_sem.at[4]),
+        pltpu.make_async_copy(gates_hbm, gates_ref, load_sem.at[5]),
     ]
     barrier = pltpu.get_barrier_semaphore()
-    peers = (sib, *y_to, *d_to, p_to, p_from)
+    peers = (sib, *y_to, *d_to, p_from)
     for peer in peers:
         pl.semaphore_signal(barrier, inc=1, device_id=peer, device_id_type=MESH)
-    for load in loads:
-        load.start()
-
+    for at in (4, 5, 0, 1, 2, 3):
+        loads[at].start()
+
+    loads[4].wait()
+    loads[5].wait()
     hit, chooser = one_hot(routing_ref[...], cap)
     share = jnp.sum(jnp.where(hit, gates_ref[...], F32(0.0)), axis=0, keepdims=True)
     weighting = jnp.sum(chooser * share, axis=1, keepdims=True)
@@ -97,86 +101,6 @@
         chosen = jnp.dot(chooser, og[:, cols], preferred_element_type=F32)
         picked[:, cols] = chosen
         rows_all[expert, :, cols] = (chosen * weighting).astype(BF16)
-    pl.semaphore_wait(barrier, len(peers))
-
-    def gather(piece, ring_send, ring_recv, sib_send, sib_recv):
-        def owner(offset):
-            return ((y + offset + n_y) % n_y) * 2 + core
-
-        def first():
-            for d, order in ((0, (0, 1)), (1, (1, 0))):
-                for h in order:
-                    send(piece(expert, h), piece(expert, h), ring_send.at[d, 0, h],
-                         ring_recv.at[d, 0, h], y_to[d])
-            for h in (0, 1):
-                send(piece(expert, h), piece(expert, h), sib_send.at[0, h], sib_recv.at[0, h], sib)
-
-        def step(k):
-            for at in (0, 1):
-                for d in (0, 1):
-                    h = at if d == 0 else 1 - at
-                    if k == far and at == 1:
-                        continue
-                    offset = -k if d == 0 else k
-                    block = piece(owner(offset), h)
-                    arrived(block, ring_recv.at[d, k - 1, h], y_to[d])
-                    if k < far - 1 or (k == far - 1 and at == 0):
-                        send(block, block, ring_send.at[d, k, h], ring_recv.at[d, k, h], y_to[d])
-                    slot = offset % n_y
-                    send(block, block, sib_send.at[slot, h], sib_recv.at[slot, h], sib)
-
-        def finish():
-            for offset in range(n_y):
-                for h in (0, 1):
-                    other = ((y + offset) % n_y) * 2 + (1 - core)
-                    arrived(piece(other, h), sib_recv.at[offset, h], sib)
-
-        return first, step, finish
-
-    ag_first, ag_step, ag_finish = gather(
-        lambda e, h: rows_all.at[e, :, pl.ds(h * half, half)], y_send, y_recv, ysib_send, ysib_recv
-    )
-    sl_first, sl_step, sl_finish = gather(
-        lambda e, h: slices.at[e, pl.ds(3 * h, 3)], s_send, s_recv, ssib_send, ssib_recv
-    )
-
-    def send_slices(src, kind):
-        for d in (0, 1):
-            peer = (dp + 1) % n_dp if d == 0 else (dp + n_dp - 1) % n_dp
-            near = pl.ds(pl.multiple_of(peer * part_d, part_d), part_d)
-            send(src.at[expert, :, near], slices.at[expert, 3 * kind + d],
-                 xy_send.at[kind, d], xy_recv.at[kind, d], d_to[d])
-            base = ((dp + 2) % n_dp) * part_d + d * (part_d // 2)
-            beyond = pl.ds(pl.multiple_of(base, part_d // 2), part_d // 2)
-            send(src.at[expert, :, beyond], relay.at[d, kind],
-                 rl_send.at[kind, d], rl_recv.at[kind, d], d_to[d])
-
-    def relay_slices(kind):
-        for d in (0, 1):
-            arrived(relay.at[d, kind], rl_recv.at[kind, d], d_to[d])
-            send(relay.at[d, kind],
-                 slices.at[expert, 3 * kind + 2, :, pl.ds(d * (part_d // 2), part_d // 2)],
-                 rf_send.at[kind, d], rf_recv.at[kind, d], d_to[d])
-
-    def slices_arrived(kind):
-        for d in (0, 1):
-            arrived(slices.at[expert, 3 * kind + d], xy_recv.at[kind, d], d_to[d])
-            arrived(slices.at[expert, 3 * kind + 2, :, pl.ds(d * (part_d // 2), part_d // 2)],
-                    rf_recv.at[kind, d], d_to[d])
-
-    og_rows = tokens // 4
-
-    def send_og(at):
-        block = pl.ds(at * og_rows, og_rows)
-        send(og_hbm.at[block], og_in.at[block], og_send.at[at], og_recv.at[at], p_to)
-
-    ag_first()
-    send_slices(x_hbm, 0)
-    send_slices(rows_all, 1)
-    send(routing_ref, routing_in, rt_send, rt_recv, p_to)
-    send(w_hbm.at[pl.ds(0, 2)], w_gu.at[core], w_send, w_recv, sib)
-    send_og(0)
-
     loads[1].wait()
     loads[2].wait()
 
@@ -189,6 +113,86 @@
         return lax.fori_loop(0, width // tile, body, jnp.zeros((out_rows, rows), F32))
 
     pre = into(lambda cols: w_gu[core, :, :, cols].reshape(2 * hid, tile), x, 2 * hid)
+    pl.semaphore_wait(barrier, len(peers))
+
+    def gather(piece, ring_send, ring_recv, sib_send, sib_recv):
+        def owner(offset):
+            return ((y + offset + n_y) % n_y) * 2 + core
+
+        def first(pieces=(0, 1)):
+            for at in range(len(pieces)):
+                for d in (0, 1):
+                    h = pieces[at if d == 0 else len(pieces) - 1 - at]
+                    send(piece(expert, h), piece(expert, h), ring_send.at[d, 0, h],
+                         ring_recv.at[d, 0, h], y_to[d])
+            for h in pieces:
+                send(piece(expert, h), piece(expert, h), sib_send.at[0, h], sib_recv.at[0, h], sib)
+
+        def step(k, pieces=(0, 1)):
+            for at in range(len(pieces)):
+                for d in (0, 1):
+                    h = pieces[at if d == 0 else len(pieces) - 1 - at]
+                    if k == far and h != d:
+                        continue
+                    offset = -k if d == 0 else k
+                    block = piece(owner(offset), h)
+                    arrived(block, ring_recv.at[d, k - 1, h], y_to[d])
+                    if k < far - 1 or (k == far - 1 and h == d):
+                        send(block, block, ring_send.at[d, k, h], ring_recv.at[d, k, h], y_to[d])
+                    slot = offset % n_y
+                    send(block, block, sib_send.at[slot, h], sib_recv.at[slot, h], sib)
+
+        def finish():
+            for offset in range(n_y):
+                for h in (0, 1):
+                    other = ((y + offset) % n_y) * 2 + (1 - core)
+                    arrived(piece(other, h), sib_recv.at[offset, h], sib)
+
+        return first, step, finish
+
+    ag_first, ag_step, ag_finish = gather(
+        lambda e, h: rows_all.at[e, :, pl.ds(h * half, half)], y_send, y_recv, ysib_send, ysib_recv
+    )
+    sl_first, sl_step, sl_finish = gather(
+        lambda e, h: slices.at[e, pl.ds(3 * h, 3)], s_send, s_recv, ssib_send, ssib_recv
+    )
+
+    def send_slices(src, kind):
+        for d in (0, 1):
+            peer = (dp + 1) % n_dp if d == 0 else (dp + n_dp - 1) % n_dp
+            near = pl.ds(pl.multiple_of(peer * part_d, part_d), part_d)
+            base = ((dp + 2) % n_dp) * part_d + d * (part_d // 2)
+            beyond = pl.ds(pl.multiple_of(base, part_d // 2), part_d // 2)
+            send(src.at[expert, :, beyond], relay.at[d, kind],
+                 rl_send.at[kind, d], rl_recv.at[kind, d], d_to[d])
+            send(src.at[expert, :, near], slices.at[expert, 3 * kind + d],
+                 xy_send.at[kind, d], xy_recv.at[kind, d], d_to[d])
+
+    def relay_slices(kind):
+        for d in (0, 1):
+            arrived(relay.at[d, kind], rl_recv.at[kind, d], d_to[d])
+            send(relay.at[d, kind],
+                 slices.at[expert, 3 * kind + 2, :, pl.ds(d * (part_d // 2), part_d // 2)],
+                 rf_send.at[kind, d], rf_recv.at[kind, d], d_to[d])
+
+    def slices_arrived(kind):
+        for d in (0, 1):
+            arrived(slices.at[expert, 3 * kind + d], xy_recv.at[kind, d], d_to[d])
+            arrived(slices.at[expert, 3 * kind + 2, :, pl.ds(d * (part_d // 2), part_d // 2)],
+                    rf_recv.at[kind, d], d_to[d])
+
+    og_pieces = 8
+    og_rows = tokens // og_pieces
+
+    def send_og(at):
+        block = pl.ds(at * og_rows, og_rows)
+        send(og_hbm.at[block], og_in.at[block], og_send.at[at], og_recv.at[at], p_to)
+
+    ag_first()
+    send_slices(x_hbm, 0)
+    send_slices(rows_all, 1)
+    send(routing_hbm, routing_in, rt_send, rt_recv, p_to)
+    send(w_hbm.at[pl.ds(0, 2)], w_gu.at[core], w_send, w_recv, sib)
     gate_pre, up_pre = pre[:hid], pre[hid:]
     sigmoid = jax.nn.sigmoid(gate_pre)
     activated = gate_pre * sigmoid
@@ -198,8 +202,6 @@
     hidden_rows = pl.ds(0, hid)
     for d in (0, 1):
         send(acts.at[hidden_rows], acts_in.at[d, hidden_rows], h_send.at[d], h_recv.at[d], d_to[d])
-    send_og(1)
-    send_og(2)
 
     def relay_hidden():
         for d in (0, 1):
@@ -209,13 +211,13 @@
 
     for k in range(1, far):
         ag_step(k)
-        if k == 1:
+        if k == far - 2:
             relay_slices(0)
-            relay_slices(1)
-    slices_arrived(0)
-    slices_arrived(1)
-    sl_first()
-    relay_hidden()
+    if far < 3:
+        relay_slices(0)
+    relay_slices(1)
+    for at in range(og_pieces // 2):
+        send_og(at)
     ag_step(far)
     ag_finish()
 
@@ -233,7 +235,11 @@
             m = at if d == 0 else 1 - at
             rows = pl.ds((1 + m) * hid, hid)
             send(acts.at[rows], acts_in.at[d, rows], g_send.at[d, m], g_recv.at[d, m], d_to[d])
-    send_og(3)
+    relay_hidden()
+    for at in range(og_pieces // 2, og_pieces):
+        send_og(at)
+    slices_arrived(0)
+    sl_first((0,))
 
     def relay_grads():
         for d in (0, 1):
@@ -269,7 +275,7 @@
              r_send.at[d, k - 1, h], r_recv.at[d, k - 1, h], y_to[d])
 
     def rs_step(k):
-        for at in (1, 0) if k == far - 1 else (0, 1):
+        for at in (0, 1):
             for d in (0, 1):
                 rs_send(d, k, at if d == 0 else 1 - at)
 
@@ -291,19 +297,28 @@
                 value = jnp.dot(left, right.reshape(-1, cell), preferred_element_type=F32)
                 acc_d[:, cols] = value if own else acc_d[:, cols] + value
 
+    sl_step(1, (0,))
     partials(0)
     rs_send(0, far, 0)
     partials(1)
     rs_send(1, far, 1)
-    sl_step(1)
+    rs_send(0, far - 1, 1)
+    rs_send(1, far - 1, 0)
+    sl_step(2, (0,))
+    slices_arrived(1)
+    sl_first((1,))
     for k in range(far - 1, 0, -1):
-        rs_step(k)
         if k == far - 1:
+            rs_send(0, k, 0)
+            rs_send(1, k, 1)
             add_grads(None, True, True)
-        if k == far - 2 or far < 3:
-            relay_grads()
-        if far - k + 1 <= far:
-            sl_step(far - k + 1)
+        else:
+            rs_step(k)
+        step = far - k
+        if step + 2 <= far:
+            sl_step(step + 2, (0,))
+        if step > 1:
+            sl_step(step - 1, (1,))
 
     for h in (0, 1):
         cols = pl.ds(h * half, half)
@@ -314,6 +329,9 @@
         final[:, cols] = (picked[:, cols] + total).astype(BF16)
         send(final.at[:, cols], final_in.at[:, cols], fin_send.at[h], fin_recv.at[h], p_to)
 
+    relay_grads()
+    for k in range(max(far - 1, 1), far + 1):
+        sl_step(k, (1,))
     sl_finish()
     for d in (0, 1):
         rows = pl.ds(d * (hid // 2), hid // 2)
@@ -331,7 +349,7 @@
     named = lax.dot_general(
         placed, jnp.ones((cap, 128), BF16), TN, preferred_element_type=F32
     )[:, 0:1] > 0.5
-    for at in range(4):
+    for at in range(og_pieces):
         block = pl.ds(at * og_rows, og_rows)
         arrived(og_in.at[block], og_recv.at[at], p_to)
     for h in (0, 1):
@@ -365,6 +383,8 @@
     DMA = pltpu.SemaphoreType.DMA
     V = pltpu.VMEM
     scratch = [
+        V(routing.shape[:1:-1], jnp.int32),
+        V(routing.shape[:1:-1], F32),
         V((tokens, width), BF16),
         V((devices, cap, width), BF16),
         V((2, 2, hid, width), BF16),
@@ -388,7 +408,7 @@
         V((hid, part_d), F32),
         V((hid, rows), F32),
         V((hid, rows), F32),
-        DMA((4,)), DMA((4,)), DMA((4,)), DMA, DMA, DMA((2,)), DMA((2,)), DMA, DMA,
+        DMA((6,)), DMA((8,)), DMA((8,)), DMA, DMA, DMA((2,)), DMA((2,)), DMA, DMA,
         DMA((2, far, 2)), DMA((2, far, 2)), DMA((n_y, 2)), DMA((n_y, 2)),
         DMA((2, far, 2)), DMA((2, far, 2)), DMA((n_y, 2)), DMA((n_y, 2)),
         DMA((2, 2)), DMA((2, 2)), DMA((2, 2)), DMA((2, 2)), DMA((2, 2)), DMA((2, 2)),
@@ -396,18 +416,18 @@
         DMA, DMA, DMA((2, far, 2)), DMA((2, far, 2)),
     ]
     vmem = pl.BlockSpec(memory_space=pltpu.VMEM)
-    anywhere = pl.BlockSpec(memory_space=pl.ANY)
+    anywhere = pl.BlockSpec(memory_space=pltpu.HBM)
     passed, grads = pl.pallas_call(
         functools.partial(kernel, n_y, n_dp, n_pipe),
         out_shape=(
-            jax.ShapeDtypeStruct((tokens, width), BF16),
-            jax.ShapeDtypeStruct((3, hid, part_d), BF16),
+            pltpu.VMEM((tokens, width), BF16),
+            pltpu.VMEM((3, hid, part_d), BF16),
         ),
-        in_specs=[vmem, vmem, anywhere, anywhere, anywhere],
+        in_specs=[anywhere] * 5,
         out_specs=(vmem, vmem),
         scratch_shapes=scratch,
         compiler_params=pltpu.CompilerParams(
-            collective_id=0, has_side_effects=True, vmem_limit_bytes=48 << 20
+            collective_id=0, has_side_effects=True
         ),
         name="expert_backward",
     )(

time: 103 us -> 89.1 us (0.87)
  the two profiles are of different devices: /device:TPU:78 before, /device:TPU:73 now
where the time goes in v2:
time: 89.1 us; the launch traced here: 88.9 us
  Pallas kernels  86.5 us (97%)
  local copies, waits for them, and re-layouts  1.79 us (2%)
    pallas_call x1, Pallas kernels, shards(): pl.pallas_call(functools.partial(kernel, n_y, n_dp, n_pipe), out_shape=(p...  86.5 us
    unnamed x2, local copies, waits for them, and re-layouts  1.79 us

profile of v2, /device:TPU:73, one launch (start us, length us, event | category | flops | bytes accessed | tf_op | source)
XLA Modules:
  0.0 88.9 jit_solution(5452638897247001047)
XLA Ops:
  0.6 86.5 %expert_backward.1 = (bf16[128,4096]{1,0:T(8,128)(2,1)S(1)}, bf16[3,96,1024]{2,1,0:T(8,128)(2,1)S(1)}) custom-call(s32[8,128]{1,0:T(8,128)} %bitcast.16, f32[8,128]{1,0:T(8,128)} %bitcast.17, bf16[128,4096]{1,0:T(8,128)(2,1)} %bitcast.15, bf16[16,16,4096]{2,1,0:T(8,128)(2,1)} %bitcast.14, bf16[3,96,4096]{2,1,0:T(8,128)(2,1)} %bitcast.13), custom_call_target="tpu_custom_call" | custom-call | tf_op jit(solution)/shard_map/expert_backward/pallas_call | solution.py:420
  87.1 1.0 %copy.9 = bf16[1,1,128,4096]{3,2,1,0:T(8,128)(2,1)} copy(bf16[1,1,128,4096]{3,2,1,0:T(8,128)(2,1)S(1)} %bitcast.11) | data formatting | bytes 2097152
  88.1 0.8 copy.10

commit v3 on v2

--- a/solution.py
+++ b/solution.py
@@ -101,18 +101,6 @@
         chosen = jnp.dot(chooser, og[:, cols], preferred_element_type=F32)
         picked[:, cols] = chosen
         rows_all[expert, :, cols] = (chosen * weighting).astype(BF16)
-    loads[1].wait()
-    loads[2].wait()
-
-    def into(weights, rows_ref, out_rows):
-        def body(at, total):
-            cols = pl.ds(pl.multiple_of(at * tile, tile), tile)
-            rows = rows_ref[:, :, cols].reshape(-1, tile)
-            return total + lax.dot_general(weights(cols), rows, NT, preferred_element_type=F32)
-        rows = rows_ref.shape[0] * rows_ref.shape[1]
-        return lax.fori_loop(0, width // tile, body, jnp.zeros((out_rows, rows), F32))
-
-    pre = into(lambda cols: w_gu[core, :, :, cols].reshape(2 * hid, tile), x, 2 * hid)
     pl.semaphore_wait(barrier, len(peers))
 
     def gather(piece, ring_send, ring_recv, sib_send, sib_recv):
@@ -193,6 +181,18 @@
     send_slices(rows_all, 1)
     send(routing_hbm, routing_in, rt_send, rt_recv, p_to)
     send(w_hbm.at[pl.ds(0, 2)], w_gu.at[core], w_send, w_recv, sib)
+    loads[1].wait()
+    loads[2].wait()
+
+    def into(weights, rows_ref, out_rows):
+        def body(at, total):
+            cols = pl.ds(pl.multiple_of(at * tile, tile), tile)
+            rows = rows_ref[:, :, cols].reshape(-1, tile)
+            return total + lax.dot_general(weights(cols), rows, NT, preferred_element_type=F32)
+        rows = rows_ref.shape[0] * rows_ref.shape[1]
+        return lax.fori_loop(0, width // tile, body, jnp.zeros((out_rows, rows), F32))
+
+    pre = into(lambda cols: w_gu[core, :, :, cols].reshape(2 * hid, tile), x, 2 * hid)
     gate_pre, up_pre = pre[:hid], pre[hid:]
     sigmoid = jax.nn.sigmoid(gate_pre)
     activated = gate_pre * sigmoid
@@ -216,8 +216,8 @@
     if far < 3:
         relay_slices(0)
     relay_slices(1)
-    for at in range(og_pieces // 2):
-        send_og(at)
+    send_og(0)
+    send_og(1)
     ag_step(far)
     ag_finish()
 
@@ -236,8 +236,6 @@
             rows = pl.ds((1 + m) * hid, hid)
             send(acts.at[rows], acts_in.at[d, rows], g_send.at[d, m], g_recv.at[d, m], d_to[d])
     relay_hidden()
-    for at in range(og_pieces // 2, og_pieces):
-        send_og(at)
     slices_arrived(0)
     sl_first((0,))
 
@@ -297,14 +295,13 @@
                 value = jnp.dot(left, right.reshape(-1, cell), preferred_element_type=F32)
                 acc_d[:, cols] = value if own else acc_d[:, cols] + value
 
-    sl_step(1, (0,))
     partials(0)
     rs_send(0, far, 0)
     partials(1)
     rs_send(1, far, 1)
     rs_send(0, far - 1, 1)
     rs_send(1, far - 1, 0)
-    sl_step(2, (0,))
+    sl_step(1, (0,))
     slices_arrived(1)
     sl_first((1,))
     for k in range(far - 1, 0, -1):
@@ -314,11 +311,13 @@
             add_grads(None, True, True)
         else:
             rs_step(k)
-        step = far - k
-        if step + 2 <= far:
-            sl_step(step + 2, (0,))
-        if step > 1:
-            sl_step(step - 1, (1,))
+        if k < far - 1:
+            sl_step(far - 1 - k, (1,))
+        sl_step(far + 1 - k, (0,))
+        if k == max(far - 2, 1):
+            relay_grads()
+            for at in range(2, og_pieces):
+                send_og(at)
 
     for h in (0, 1):
         cols = pl.ds(h * half, half)
@@ -329,8 +328,7 @@
         final[:, cols] = (picked[:, cols] + total).astype(BF16)
         send(final.at[:, cols], final_in.at[:, cols], fin_send.at[h], fin_recv.at[h], p_to)
 
-    relay_grads()
-    for k in range(max(far - 1, 1), far + 1):
+    for k in range(far - 1, far + 1):
         sl_step(k, (1,))
     sl_finish()
     for d in (0, 1):
@@ -342,6 +340,14 @@
         rows = pl.ds((2 - d) * hid, hid)
         arrived(acts_in.at[d, rows], g_recv.at[d, 1 - d], d_to[d])
         add_grads(d, True, False)
+
+    for d in (0, 1):
+        rows = pl.ds((1 + d) * hid, hid)
+        arrived(acts_in.at[2, rows], gf_recv.at[d], d_to[d])
+    add_grads(2, True, False)
+    grads_ref[0] = acc_gu[0:hid, :].astype(BF16)
+    grads_ref[1] = acc_gu[hid:2 * hid, :].astype(BF16)
+    grads_ref[2] = acc_d[...].astype(BF16)
 
     arrived(routing_in, rt_recv, p_to)
     _, placed = one_hot(routing_in[...], cap)
@@ -359,13 +365,6 @@
         value = lax.dot_general(placed, final_in[:, cols], TN, preferred_element_type=F32)
         passed_ref[:, cols] = jnp.where(named, value, og_in[:, cols].astype(F32)).astype(BF16)
 
-    for d in (0, 1):
-        rows = pl.ds((1 + d) * hid, hid)
-        arrived(acts_in.at[2, rows], gf_recv.at[d], d_to[d])
-    add_grads(2, True, False)
-    grads_ref[0] = acc_gu[0:hid, :].astype(BF16)
-    grads_ref[1] = acc_gu[hid:2 * hid, :].astype(BF16)
-    grads_ref[2] = acc_d[...].astype(BF16)
     for copy in sent:
         copy.wait_send()
 

time: 89.1 us -> 84.8 us (0.952)
  the two profiles are of different devices: /device:TPU:73 before, /device:TPU:70 now
where the time goes in v3:
time: 84.8 us; the launch traced here: 84.6 us
  Pallas kernels  82.2 us (97%)
  local copies, waits for them, and re-layouts  1.79 us (2%)
    pallas_call x1, Pallas kernels, shards(): pl.pallas_call(functools.partial(kernel, n_y, n_dp, n_pipe), out_shape=(p...  82.2 us
    unnamed x2, local copies, waits for them, and re-layouts  1.79 us

profile of v3, /device:TPU:70, one launch (start us, length us, event | category | flops | bytes accessed | tf_op | source)
XLA Modules:
  0.0 84.6 jit_solution(3673130703697505335)
XLA Ops:
  0.6 82.2 %expert_backward.1 = (bf16[128,4096]{1,0:T(8,128)(2,1)S(1)}, bf16[3,96,1024]{2,1,0:T(8,128)(2,1)S(1)}) custom-call(s32[8,128]{1,0:T(8,128)} %bitcast.16, f32[8,128]{1,0:T(8,128)} %bitcast.17, bf16[128,4096]{1,0:T(8,128)(2,1)} %bitcast.15, bf16[16,16,4096]{2,1,0:T(8,128)(2,1)} %bitcast.14, bf16[3,96,4096]{2,1,0:T(8,128)(2,1)} %bitcast.13), custom_call_target="tpu_custom_call" | custom-call | tf_op jit(solution)/shard_map/expert_backward/pallas_call | solution.py:419
  82.8 1.0 %copy.9 = bf16[1,1,128,4096]{3,2,1,0:T(8,128)(2,1)} copy(bf16[1,1,128,4096]{3,2,1,0:T(8,128)(2,1)S(1)} %bitcast.11) | data formatting | bytes 2097152
  83.8 0.8 copy.10

commit v4 on v3

--- a/solution.py
+++ b/solution.py
@@ -26,6 +26,19 @@
     slot = jnp.dot(rows.astype(BF16), upper, preferred_element_type=F32)
     index = lax.broadcasted_iota(jnp.int32, (capacity, tokens), 0).astype(F32)
     return hit, jnp.where((slot == index) & (rows > 0.5), F32(1.0), F32(0.0))
+
+
+def write_out(passed_ref, grads_ref, passed_hbm, grads_hbm, sems):
+    half = passed_ref.shape[0] // 2
+    copies = [
+        pltpu.make_async_copy(passed_ref.at[pl.ds(0, half)], passed_hbm.at[pl.ds(0, half)], sems.at[0]),
+        pltpu.make_async_copy(passed_ref.at[pl.ds(half, half)], passed_hbm.at[pl.ds(half, half)], sems.at[1]),
+        pltpu.make_async_copy(grads_ref, grads_hbm, sems.at[2]),
+    ]
+    for copy in copies:
+        copy.start()
+    for copy in copies:
+        copy.wait()
 
 
 def kernel(
@@ -316,8 +329,11 @@
         sl_step(far + 1 - k, (0,))
         if k == max(far - 2, 1):
             relay_grads()
-            for at in range(2, og_pieces):
-                send_og(at)
+            send_og(2)
+            send_og(3)
+        if k == 1:
+            send_og(4)
+            send_og(5)
 
     for h in (0, 1):
         cols = pl.ds(h * half, half)
@@ -328,6 +344,8 @@
         final[:, cols] = (picked[:, cols] + total).astype(BF16)
         send(final.at[:, cols], final_in.at[:, cols], fin_send.at[h], fin_recv.at[h], p_to)
 
+    send_og(6)
+    send_og(7)
     for k in range(far - 1, far + 1):
         sl_step(k, (1,))
     sl_finish()
@@ -436,6 +454,18 @@
         saved_inputs[0, 0, 0],
         expert_weights[0],
     )
+    passed, grads = pl.pallas_call(
+        write_out,
+        out_shape=(
+            jax.ShapeDtypeStruct((tokens, width), BF16),
+            jax.ShapeDtypeStruct((3, hid, part_d), BF16),
+        ),
+        in_specs=[vmem, vmem],
+        out_specs=(anywhere, anywhere),
+        scratch_shapes=[DMA((3,))],
+        compiler_params=pltpu.CompilerParams(vmem_limit_bytes=8 << 20),
+        name="write_out",
+    )(passed, grads)
     return passed[None, None], grads[None]
 
 

time: 84.8 us -> 84.2 us (level)
  local copies, waits for them, and re-layouts: 1.79 us -> 0 us
  Pallas kernels: 82.2 us -> 83.4 us
    unnamed x2 -> x0, local copies, waits for them, and re-layouts: 1.79 us -> none
    pallas_call x0 -> x1, Pallas kernels: none -> 1.19 us  [shards(): pl.pallas_call(write_out, out_shape=(jax.ShapeDtypeStruct((tokens, width)...]
where the time goes in v4:
time: 84.2 us; the launch traced here: 84 us
  Pallas kernels  83.4 us (99%)
    pallas_call x1, Pallas kernels, shards(): pl.pallas_call(functools.partial(kernel, n_y, n_dp, n_pipe), out_shape=(p...  82.2 us

profile of v4, /device:TPU:70, one launch (start us, length us, event | category | flops | bytes accessed | tf_op | source)
XLA Modules:
  0.0 84.0 jit_solution(2560298452367502328)
XLA Ops:
  0.6 82.2 %expert_backward.1 = (bf16[128,4096]{1,0:T(8,128)(2,1)S(1)}, bf16[3,96,1024]{2,1,0:T(8,128)(2,1)S(1)}) custom-call(s32[8,128]{1,0:T(8,128)} %bitcast.14, f32[8,128]{1,0:T(8,128)} %bitcast.15, bf16[128,4096]{1,0:T(8,128)(2,1)} %bitcast.13, bf16[16,16,4096]{2,1,0:T(8,128)(2,1)} %bitcast.12, bf16[3,96,4096]{2,1,0:T(8,128)(2,1)} %bitcast.11), custom_call_target="tpu_custom_call" | custom-call | tf_op jit(solution)/shard_map/expert_backward/pallas_call | solution.py:437
  82.8 1.2 %write_out.1 = (bf16[128,4096]{1,0:T(8,128)(2,1)}, bf16[3,96,1024]{2,1,0:T(8,128)(2,1)}) custom-call(bf16[128,4096]{1,0:T(8,128)(2,1)S(1)} %get-tuple-element.6.passed_ref, bf16[3,96,1024]{2,1,0:T(8,128)(2,1)S(1)} %get-tuple-element.7.grads_ref), custom_call_target="tpu_custom_call" | custom-call | tf_op jit(solution)/shard_map/write_out/pallas_call | solution.py:457
